TPU v7x, 32 devices: a whole 2x2x4 slice. The times are simulated.
32 devices in a mesh: groups: 2 (over y), qry: 4 (over x, core), ref: 4 (over z).
Axes of the slice: x: 2, y: 2, z: 4, core: 2. Of those that a mesh axis runs over, the one named last changes fastest.
Arguments:
- query_feats: bfloat16 [1024, 9, 3840], P(('groups', 'qry')), parts along dimension 0, may hold values from -6 to 6
- ref_feats: bfloat16 [256, 4, 9, 3840], P(('groups', 'ref'), 'qry'), parts along dimension 0, may hold values from -6 to 6
- pair_table: int32 [8, 4], P('groups'), parts along dimension 0, may hold values from 0 to 1, as said below
- lengths: int32 [4], P('groups'), parts along dimension 0, may hold values from 1 to 96, 128 in all
- query_len: int32 [2], P('groups'), parts along dimension 0, may hold values from 64 to 128
- conv1_weight: float32 [3, 3, 32], replicated, may hold values from -2 to 2
- conv1_bias: float32 [32], replicated, may hold values from -3 to 3
- conv2_weight: bfloat16 [3, 3, 64, 32], replicated, may hold values from -0.375 to 0.375
- conv2_bias: float32 [64], replicated, may hold values from -3 to 3
- conv3_weight: bfloat16 [3, 3, 128, 64], replicated, may hold values from -0.25 to 0.25
- conv3_bias: float32 [128], replicated, may hold values from -3 to 3
- conv4_weight: bfloat16 [128], replicated, may hold values from -0.5 to 0.5
- conv4_bias: float32 [1], replicated, may hold values from -3 to 3
Outputs:
- score_map: float32 [256, 128], P(('groups', 'qry'), 'ref'), parts along dimension 0
- video_scores: float32 [4], P('groups'), parts along dimension 0
There are 2 independent parts, one for each index of `groups`. A program takes and returns all parts, laid end to end along the dimension named above; an argument that names none is the same for every part. Nothing has to cross between parts.
Inputs may be any that keep to these rules, and one draw needn't show every extreme that they name: `pair_table`: in each row, at most 1 of the 1 tiles in the block of one index of ref are 1, and some such block holds exactly 1 in every draw.
All inputs are finite; a program needn't handle non-finite values.
Results may differ from a plain program's by a relative error of at most 0.01.
Values may be sent and summed in bfloat16 or wider, within the bound.
No kernel may reach another device: no remote copies, remote signals or barrier semaphores. Data moves between devices by JAX's collectives and lax.ppermute only.
A program may use at most 128 MiB of HBM per device.

v0:
```python
import math
import jax
import jax.numpy as jnp
from jax import lax
from jax.sharding import PartitionSpec as P

MOST = 1


def padded_2(block, sides, width):
    for axis, dim in sides:
        count = lax.axis_size(axis)
        forward = [(i, i + 1) for i in range(count - 1)]
        backward = [(target, source) for source, target in forward]
        low = lax.ppermute(
            lax.slice_in_dim(block, block.shape[dim] - width, None, axis=dim), axis, forward
        )
        high = lax.ppermute(lax.slice_in_dim(block, 0, width, axis=dim), axis, backward)
        block = jnp.concatenate([low, block, high], axis=dim)
    return block


def slot_table(mask, most):
    width = mask.shape[-1]
    ranking = jnp.cumsum(mask, axis=-1) - 1
    slot_ids = jnp.arange(most, dtype=jnp.int32)
    chosen = (mask[..., None, :] == 1) & (ranking[..., None, :] == slot_ids[:, None])
    picked = jnp.sum(jnp.where(chosen, jnp.arange(width, dtype=jnp.int32), 0), axis=-1)
    return (chosen, picked)


def frame_sims(query_mat, ref_mat, regions):
    products = lax.dot_general(
        query_mat, ref_mat, (((1,), (1,)), ((), ())), preferred_element_type=jnp.float32
    )
    frames = query_mat.shape[0] // regions
    others = ref_mat.shape[0] // regions
    best = jnp.max(products.reshape(frames, regions, others, regions), axis=3)
    return jnp.sum(best, axis=1) * (1.0 / (regions * math.sqrt(query_mat.shape[1])))


def conv_layer(padded, weights, bias, block_rows, use_pool):
    channels = padded.shape[0]
    height = padded.shape[1] - 2
    width = padded.shape[2] - 2
    block_rows = math.gcd(height, block_rows)
    outputs = weights.shape[0]
    accuracy = lax.Precision.HIGHEST if padded.dtype == jnp.float32 else None

    def one_block(position):
        window = lax.dynamic_slice_in_dim(padded, position * block_rows, block_rows + 2, 1)
        stacked = jnp.concatenate(
            [
                window[:, shift_row : shift_row + block_rows, shift_col : shift_col + width]
                for shift_row in range(3)
                for shift_col in range(3)
            ],
            axis=0,
        )
        result = jnp.dot(
            weights,
            stacked.reshape(9 * channels, block_rows * width),
            preferred_element_type=jnp.float32,
            precision=accuracy,
        )
        result = (result + bias[:, None]).reshape(outputs, block_rows, width)
        result = jnp.maximum(result, 0.0)
        if use_pool:
            result = jnp.max(
                result.reshape(outputs, block_rows // 2, 2, width // 2, 2), axis=(2, 4)
            )
        return result

    blocks = lax.map(one_block, jnp.arange(height // block_rows, dtype=jnp.int32))
    return jnp.transpose(blocks, (1, 0, 2, 3)).reshape(outputs, -1, blocks.shape[-1])


def weight_matrix(weight):
    return jnp.transpose(weight, (2, 0, 1, 3)).reshape(weight.shape[2], -1)


def body(
    query_feats,
    ref_feats,
    pair_table,
    lengths,
    query_len,
    conv1_weight,
    conv1_bias,
    conv2_weight,
    conv2_bias,
    conv3_weight,
    conv3_bias,
    conv4_weight,
    conv4_bias,
):
    qry_index = lax.axis_index("qry")
    ref_index = lax.axis_index("ref")
    frames = query_feats.shape[0]
    regions = query_feats.shape[1]
    channels = query_feats.shape[2]
    tiles_here = pair_table.shape[1] // lax.axis_size("ref")
    tile_rows = ref_feats.shape[0] // tiles_here
    query_mat = query_feats.reshape(frames * regions, channels)
    own_mask = lax.dynamic_slice(pair_table, (qry_index, ref_index * tiles_here), (1, tiles_here))[
        0
    ]
    chosen, picked = slot_table(own_mask, MOST)
    shards = lax.all_gather(ref_feats, "qry", axis=1, tiled=True)
    senders = shards.shape[1]
    sims = frame_sims(query_mat, shards.reshape(tile_rows * senders * regions, channels), regions)
    sims = sims.reshape(1, frames, tile_rows, senders)
    tile_sims = sims.reshape(MOST, frames, frames)
    placed = jnp.einsum(
        "st,sqf->qtf", chosen.astype(jnp.float32), tile_sims, precision=lax.Precision.HIGHEST
    )
    sim_map = placed.reshape(frames, tiles_here * frames)
    padded = padded_2(sim_map, (("qry", 0), ("ref", 1)), 1)
    first_weights = jnp.transpose(conv1_weight, (2, 0, 1)).reshape(conv1_weight.shape[2], 9)
    first = conv_layer(padded[None], first_weights, conv1_bias, 32, True).astype(jnp.bfloat16)
    padded = padded_2(first, (("qry", 1), ("ref", 2)), 1)
    second = conv_layer(padded, weight_matrix(conv2_weight), conv2_bias, 16, True).astype(
        jnp.bfloat16
    )
    padded = padded_2(second, (("qry", 1), ("ref", 2)), 1)
    third = conv_layer(padded, weight_matrix(conv3_weight), conv3_bias, 16, False).astype(
        jnp.bfloat16
    )
    map_rows = third.shape[1]
    map_cols = third.shape[2]
    score_map = (
        jnp.dot(
            conv4_weight[None],
            third.reshape(third.shape[0], -1),
            preferred_element_type=jnp.float32,
        ).reshape(map_rows, map_cols)
        + conv4_bias[0]
    )
    ends = jnp.cumsum(lengths)
    starts = ends - lengths
    column = ref_index * map_cols + jnp.arange(map_cols, dtype=jnp.int32)
    member = (column[:, None] >= starts[None, :]) & (column[:, None] < ends[None, :])
    peaks = jnp.max(jnp.where(member[None], score_map[:, :, None], -jnp.inf), axis=1)
    peaks = lax.pmax(peaks, "ref")
    row_ids = qry_index * map_rows + jnp.arange(map_rows, dtype=jnp.int32)
    partial_value = jnp.sum(jnp.where((row_ids < query_len[0])[:, None], peaks, 0.0), axis=0)
    totals = lax.psum(partial_value, "qry")
    return (score_map, totals / query_len[0].astype(jnp.float32))


def solution(mesh):
    placed = (
        P(("groups", "qry"), None, None),
        P(("groups", "ref"), "qry", None, None),
        P("groups", None),
        P("groups"),
        P("groups"),
        P(),
        P(),
        P(),
        P(),
        P(),
        P(),
        P(),
        P(),
    )
    return jax.shard_map(
        body,
        mesh=mesh,
        in_specs=placed,
        out_specs=(P(("groups", "qry"), "ref"), P("groups")),
        check_vma=False,
    )
```

profile of v0, /device:TPU:0, one launch (start us, length us, event | category | flops | bytes accessed | tf_op | source)
XLA Modules:
  0.0 248.4 jit_solution(3101193552977106752)
XLA Ops:
  10.5 62.7 %all-gather.2.cloned.1.call-done = bf16[32,4,9,3840]{3,0,2,1:T(8,128)(2,1)} async-done(((bf16[32,1,9,3840]{3,0,2,1:T(8,128)(2,1)}), bf16[32,4,9,3840]{3,0,2,1:T(8,128)(2,1)}) %all-gather.2.cloned.1.call-update) | async-done | bytes 8847376 | tf_op jit(solution)/shard_map/all_gather | solution.py:109
  73.2 8.6 %copy.62 = bf16[32,4,9,3840]{3,1,0,2:T(4,128)(2,1)} copy(bf16[32,4,9,3840]{3,0,2,1:T(8,128)(2,1)} %all-gather.2.cloned.1.call-done) | data formatting | bytes 17694720 | tf_op jit(solution)/shard_map/all_gather | solution.py:109
  81.8 12.7 %reshape.195 = bf16[128,9,3840,1]{2,0,1,3:T(8,128)(2,1)} reshape(bf16[32,4,9,3840]{3,1,0,2:T(4,128)(2,1)} %copy.62) | data formatting | bytes 17694720 | tf_op jit(solution)/shard_map/dot_general | solution.py:33
  94.5 18.8 %fusion.7 = f32[128,9,128]{2,0,1:T(8,128)S(1)} fusion(bf16[128,9,3840,1]{2,0,1,3:T(8,128)(2,1)} %reshape.195, bf16[128,9,3840]{2,0,1:T(8,128)(2,1)} %param.19), kind=kOutput, calls=%fused_computation.40 | convolution fusion | flops 10193338368 | bytes 18284544 | tf_op jit(solution)/shard_map/dot_general | solution.py:33
  118.7 3.4 %collective-permute-start.2 = (f32[130,1]{1,0:T(8,128)S(1)}, f32[130,1]{1,0:T(8,128)S(1)}, u32[]{:S(2)}, u32[]{:S(2)}) collective-permute-start(f32[130,1]{1,0:T(8,128)S(1)} %get-tuple-element.223), channel_id=1, source_target_pairs={{0,1},{1,2},{2,3},{4,5},{5,6},{6,7},{8,9},{9,10},{10,11},{12,13},{... | collective-permute-start | bytes 1568 | tf_op jit(solution)/shard_map/ppermute | solution.py:15
  124.1 4.3 %collective-permute-done.3 = f32[130,1]{1,0:T(8,128)S(1)} collective-permute-done((f32[130,1]{1,0:T(8,128)S(1)}, f32[130,1]{1,0:T(8,128)S(1)}, u32[]{:S(2)}, u32[]{:S(2)}) %collective-permute-start.3) | collective-permute-done | bytes 552 | tf_op jit(solution)/shard_map/ppermute | solution.py:18
  128.5 23.2 %while.30 = (s32[]{:T(128)}, bf16[4,32,16,64]{3,2,0,1:T(8,128)(2,1)S(1)}, s32[4]{0:T(128)S(1)}, f32[1,130,130]{2,1,0:T(8,128)S(1)}, f32[32,9]{0,1:T(8,128)S(1)},...) while((s32[]{:T(128)}, ...), condition=%wide.region_4.5_spmd, body=%wide.region_2.4_spmd.sunk | while | flops 14647306 | bytes 2885173 | solution.py:74
  131.6 2.5 %reduce_max.42 = bf16[32,16,64]{0,2,1:T(8,128)(2,1)S(1)} reduce(bf16[32,16,2,64,2]{0,4,3,2,1:T(2,128)(2,1)S(1)} %bitcast.115, bf16[]{:T(256)} %constant.179..sunk), dimensions={2,4}, to_apply=%region_3.3 | reduce | flops 98304 | bytes 327682 | tf_op jit(solution)/shard_map/while/body/eval_jaxpr/reduce_max | solution.py:69
  137.4 2.5 %reduce_max.42 = bf16[32,16,64]{0,2,1:T(8,128)(2,1)S(1)} reduce(bf16[32,16,2,64,2]{0,4,3,2,1:T(2,128)(2,1)S(1)} %bitcast.115, bf16[]{:T(256)} %constant.179..sunk), dimensions={2,4}, to_apply=%region_3.3 | reduce | flops 98304 | bytes 327682 | tf_op jit(solution)/shard_map/while/body/eval_jaxpr/reduce_max | solution.py:69
  143.2 2.5 %reduce_max.42 = bf16[32,16,64]{0,2,1:T(8,128)(2,1)S(1)} reduce(bf16[32,16,2,64,2]{0,4,3,2,1:T(2,128)(2,1)S(1)} %bitcast.115, bf16[]{:T(256)} %constant.179..sunk), dimensions={2,4}, to_apply=%region_3.3 | reduce | flops 98304 | bytes 327682 | tf_op jit(solution)/shard_map/while/body/eval_jaxpr/reduce_max | solution.py:69
  149.0 2.5 %reduce_max.42 = bf16[32,16,64]{0,2,1:T(8,128)(2,1)S(1)} reduce(bf16[32,16,2,64,2]{0,4,3,2,1:T(2,128)(2,1)S(1)} %bitcast.115, bf16[]{:T(256)} %constant.179..sunk), dimensions={2,4}, to_apply=%region_3.3 | reduce | flops 98304 | bytes 327682 | tf_op jit(solution)/shard_map/while/body/eval_jaxpr/reduce_max | solution.py:69
  151.7 2.7 %collective-permute-start.4 = (bf16[32,1,64]{2,1,0:T(2,128)(2,1)S(1)}, bf16[32,1,64]{2,1,0:T(2,128)(2,1)S(1)}, u32[]{:S(2)}, u32[]{:S(2)}) collective-permute-start(bf16[32,1,64]{2,1,0:T(2,128)(2,1)S(1)} %get-tuple-element.217), channel_id=1, source_target_pairs={{0,4},{4,8},{8,12},{1,5},{5,9},{9,13},{2,6},{6,10},{10,14},{3,7},{... | collective-permute-start | bytes 12296 | tf_op jit(solution)/shard_map/ppermute | solution.py:15
  155.8 2.7 %collective-permute-done.5 = bf16[32,1,64]{2,1,0:T(2,128)(2,1)S(1)} collective-permute-done((bf16[32,1,64]{2,1,0:T(2,128)(2,1)S(1)}, bf16[32,1,64]{2,1,0:T(2,128)(2,1)S(1)}, u32[]{:S(2)}, u32[]{:S(2)}) %collective-permute-start.5) | collective-permute-done | bytes 4128 | tf_op jit(solution)/shard_map/ppermute | solution.py:18
  159.3 3.4 %collective-permute-start.6 = (bf16[32,66,1]{1,0,2:T(8,128)(2,1)S(1)}, bf16[32,66,1]{1,0,2:T(8,128)(2,1)S(1)}, u32[]{:S(2)}, u32[]{:S(2)}) collective-permute-start(bf16[32,66,1]{1,0,2:T(8,128)(2,1)S(1)} %copy.64), channel_id=1, source_target_pairs={{0,1},{1,2},{2,3},{4,5},{5,6},{6,7},{8,9},{9,10},{10,11},{12,13},{... | collective-permute-start | bytes 12680 | tf_op jit(solution)/shard_map/ppermute | solution.py:15
  165.7 2.9 %collective-permute-done.7 = bf16[32,66,1]{1,0,2:T(8,128)(2,1)S(1)} collective-permute-done((bf16[32,66,1]{1,0,2:T(8,128)(2,1)S(1)}, bf16[32,66,1]{1,0,2:T(8,128)(2,1)S(1)}, u32[]{:S(2)}, u32[]{:S(2)}) %collective-permute-start.7) | collective-permute-done | bytes 4256 | tf_op jit(solution)/shard_map/ppermute | solution.py:18
  170.1 32.3 %while.31 = (s32[]{:T(128)}, bf16[4,64,8,32]{1,3,2,0:T(8,128)(2,1)}, s32[4]{0:T(128)S(1)}, bf16[32,66,66]{2,0,1:T(8,128)(2,1)S(1)}, bf16[64,288]{1,0:T(8,128)(2,...) while((s32[]{:T(128)}, ...), condition=%wide.region_7.8_spmd, body=%wide.region_5.7_spmd.sunk | while | flops 37994504 | bytes 4822013 | solution.py:74
  174.0 2.4 concatenate.35
  182.1 2.4 concatenate.35
  203.1 2.9 %collective-permute-start.8 = (bf16[64,1,32]{0,2,1:T(8,128)(2,1)S(1)}, bf16[64,1,32]{0,2,1:T(8,128)(2,1)S(1)}, u32[]{:S(2)}, u32[]{:S(2)}) collective-permute-start(bf16[64,1,32]{0,2,1:T(8,128)(2,1)S(1)} %get-tuple-element.221), channel_id=1, source_target_pairs={{0,4},{4,8},{8,12},{1,5},{5,9},{9,13},{2,6},{6,10},{10,14},{3,7},{... | collective-permute-start | bytes 12296 | tf_op jit(solution)/shard_map/ppermute | solution.py:15
  211.0 3.4 %collective-permute-start.10 = (bf16[64,34,1]{0,2,1:T(2,128)(2,1)S(1)}, bf16[64,34,1]{0,2,1:T(2,128)(2,1)S(1)}, u32[]{:S(2)}, u32[]{:S(2)}) collective-permute-start(bf16[64,34,1]{0,2,1:T(2,128)(2,1)S(1)} %get-tuple-element.219), channel_id=1, source_target_pairs={{0,1},{1,2},{2,3},{4,5},{5,6},{6,7},{8,9},{9,10},{10,11},{12,13},{... | collective-permute-start | bytes 13064 | tf_op jit(solution)/shard_map/ppermute | solution.py:15
  217.5 2.6 %collective-permute-done.11 = bf16[64,34,1]{0,2,1:T(2,128)(2,1)S(1)} collective-permute-done((bf16[64,34,1]{0,2,1:T(2,128)(2,1)S(1)}, bf16[64,34,1]{0,2,1:T(2,128)(2,1)S(1)}, u32[]{:S(2)}, u32[]{:S(2)}) %collective-permute-start.11) | collective-permute-done | bytes 4384 | tf_op jit(solution)/shard_map/ppermute | solution.py:18
  221.2 4.8 %while.32 = (s32[]{:T(128)}, bf16[2,128,16,32]{1,3,2,0:T(8,128)(2,1)S(1)}, s32[2]{0:T(128)S(1)}, bf16[64,34,34]{0,2,1:T(8,128)(2,1)S(1)}, bf16[128,576]{1,0:T(8,...) while((s32[]{:T(128)}, ...), condition=%wide.region_9.10_spmd, body=%wide.region_8.9_spmd.sunk | while | flops 75694088 | bytes 3490551 | solution.py:74
  226.6 8.5 %pmax.7 = f32[32,2]{0,1:T(2,128)S(1)} all-reduce(f32[32,2]{0,1:T(2,128)S(1)} %select_reduce_fusion), channel_id=1, replica_groups=mesh['groups'=2,'qry'=4,'ref'=4] {'ref'}, use_global_device_ids=true, to_apply=%region_12.13 | all-reduce | flops 64 | bytes 512 | tf_op jit(solution)/shard_map/pmax | solution.py:144
  235.2 5.8 %psum.7 = f32[2]{0:T(128)S(1)} all-reduce(f32[2]{0:T(128)S(1)} %select_reduce_fusion.1), channel_id=1, replica_groups=mesh['groups'=2,'qry'=4,'ref'=4] {'qry'}, use_global_device_ids=true, to_apply=%region_14.15 | all-reduce | flops 2 | bytes 16 | tf_op jit(solution)/shard_map/psum | solution.py:147
  (207 shorter events, 63.9 us)
Async XLA Ops:
  7.2 218.9 %copy-start = (bf16[128]{0:T(256)(128)(2,1)S(1)}, bf16[128]{0:T(256)(128)(2,1)}, u32[]{:S(2)}) copy-start(bf16[128]{0:T(256)(128)(2,1)} %param.30) | copy-start | bytes 772
  7.2 66.0 %all-gather.2.cloned.1.call-start = ((), (), s32[]{:S(2)}) async-start(), calls=%async_computation | async-start | bytes 11059200 | tf_op jit(solution)/shard_map/all_gather | solution.py:109
  94.5 28.9 %copy-start.6 = (f32[3,3,32]{2,1,0:T(4,128)S(1)}, f32[3,3,32]{2,1,0:T(4,128)}, u32[]{:S(2)}) copy-start(f32[3,3,32]{2,1,0:T(4,128)} %param.24) | copy-start | bytes 3460
  94.5 29.0 %copy-start.7 = (s32[2]{0:T(128)S(1)}, s32[2]{0:T(128)}, u32[]{:S(2)}) copy-start(s32[2]{0:T(128)} %param.22) | copy-start | bytes 28
  94.5 34.0 %copy-start.5 = (f32[32]{0:T(128)S(1)}, f32[32]{0:T(128)}, u32[]{:S(2)}) copy-start(f32[32]{0:T(128)} %param.25) | copy-start | bytes 388
  113.4 3.5 %collective-permute-start = (f32[1,128]{1,0:T(1,128)S(1)}, f32[1,128]{1,0:T(1,128)S(1)}, u32[]{:S(2)}, u32[]{:S(2)}) collective-permute-start(f32[1,128]{1,0:T(1,128)S(1)} %get-tuple-element.225), channel_id=1, source_target_pairs={{0,4},{4,8},{8,12},{1,5},{5,9},{9,13},{2,6},{6,10},{10,14},{3,7},{... | collective-permute-start | bytes 1544 | tf_op jit(solution)/shard_map/ppermute | solution.py:15
  115.6 3.1 %collective-permute-start.1 = (f32[1,128]{1,0:T(1,128)S(1)}, f32[1,128]{1,0:T(1,128)S(1)}, u32[]{:S(2)}, u32[]{:S(2)}) collective-permute-start(f32[1,128]{1,0:T(1,128)S(1)} %get-tuple-element.226), channel_id=1, source_target_pairs={{4,0},{8,4},{12,8},{5,1},{9,5},{13,9},{6,2},{10,6},{14,10},{7,3},{... | collective-permute-start | bytes 1544 | tf_op jit(solution)/shard_map/ppermute | solution.py:18
  118.7 5.3 %collective-permute-start.2 = (f32[130,1]{1,0:T(8,128)S(1)}, f32[130,1]{1,0:T(8,128)S(1)}, u32[]{:S(2)}, u32[]{:S(2)}) collective-permute-start(f32[130,1]{1,0:T(8,128)S(1)} %get-tuple-element.223), channel_id=1, source_target_pairs={{0,1},{1,2},{2,3},{4,5},{5,6},{6,7},{8,9},{9,10},{10,11},{12,13},{... | collective-permute-start | bytes 1568 | tf_op jit(solution)/shard_map/ppermute | solution.py:15
  122.1 6.2 %collective-permute-start.3 = (f32[130,1]{1,0:T(8,128)S(1)}, f32[130,1]{1,0:T(8,128)S(1)}, u32[]{:S(2)}, u32[]{:S(2)}) collective-permute-start(f32[130,1]{1,0:T(8,128)S(1)} %get-tuple-element.224), channel_id=1, source_target_pairs={{1,0},{2,1},{3,2},{5,4},{6,5},{7,6},{9,8},{10,9},{11,10},{13,12},{... | collective-permute-start | bytes 1568 | tf_op jit(solution)/shard_map/ppermute | solution.py:18
  128.5 36.1 %copy-start.1 = (bf16[3,3,64,32]{2,3,1,0:T(8,128)(2,1)S(1)}, bf16[3,3,64,32]{2,3,1,0:T(8,128)(2,1)}, u32[]{:S(2)}) copy-start(bf16[3,3,64,32]{2,3,1,0:T(8,128)(2,1)} %param.26) | copy-start | bytes 110596
  151.7 18.4 %copy-start.3 = (f32[64]{0:T(128)S(1)}, f32[64]{0:T(128)}, u32[]{:S(2)}) copy-start(f32[64]{0:T(128)} %param.27) | copy-start | bytes 772
  151.7 4.1 %collective-permute-start.4 = (bf16[32,1,64]{2,1,0:T(2,128)(2,1)S(1)}, bf16[32,1,64]{2,1,0:T(2,128)(2,1)S(1)}, u32[]{:S(2)}, u32[]{:S(2)}) collective-permute-start(bf16[32,1,64]{2,1,0:T(2,128)(2,1)S(1)} %get-tuple-element.217), channel_id=1, source_target_pairs={{0,4},{4,8},{8,12},{1,5},{5,9},{9,13},{2,6},{6,10},{10,14},{3,7},{... | collective-permute-start | bytes 12296 | tf_op jit(solution)/shard_map/ppermute | solution.py:15
  154.5 4.1 %collective-permute-start.5 = (bf16[32,1,64]{2,1,0:T(2,128)(2,1)S(1)}, bf16[32,1,64]{2,1,0:T(2,128)(2,1)S(1)}, u32[]{:S(2)}, u32[]{:S(2)}) collective-permute-start(bf16[32,1,64]{2,1,0:T(2,128)(2,1)S(1)} %get-tuple-element.218), channel_id=1, source_target_pairs={{4,0},{8,4},{12,8},{5,1},{9,5},{13,9},{6,2},{10,6},{14,10},{7,3},{... | collective-permute-start | bytes 12296 | tf_op jit(solution)/shard_map/ppermute | solution.py:18
  159.3 5.4 %collective-permute-start.6 = (bf16[32,66,1]{1,0,2:T(8,128)(2,1)S(1)}, bf16[32,66,1]{1,0,2:T(8,128)(2,1)S(1)}, u32[]{:S(2)}, u32[]{:S(2)}) collective-permute-start(bf16[32,66,1]{1,0,2:T(8,128)(2,1)S(1)} %copy.64), channel_id=1, source_target_pairs={{0,1},{1,2},{2,3},{4,5},{5,6},{6,7},{8,9},{9,10},{10,11},{12,13},{... | collective-permute-start | bytes 12680 | tf_op jit(solution)/shard_map/ppermute | solution.py:15
  163.1 5.5 %collective-permute-start.7 = (bf16[32,66,1]{1,0,2:T(8,128)(2,1)S(1)}, bf16[32,66,1]{1,0,2:T(8,128)(2,1)S(1)}, u32[]{:S(2)}, u32[]{:S(2)}) collective-permute-start(bf16[32,66,1]{1,0,2:T(8,128)(2,1)S(1)} %copy.65), channel_id=1, source_target_pairs={{1,0},{2,1},{3,2},{5,4},{6,5},{7,6},{9,8},{10,9},{11,10},{13,12},{... | collective-permute-start | bytes 12680 | tf_op jit(solution)/shard_map/ppermute | solution.py:18
  170.1 51.1 %copy-start.4 = (f32[128]{0:T(128)S(1)}, f32[128]{0:T(128)}, u32[]{:S(2)}) copy-start(f32[128]{0:T(128)} %param.29) | copy-start | bytes 1540
  203.1 5.0 %collective-permute-start.8 = (bf16[64,1,32]{0,2,1:T(8,128)(2,1)S(1)}, bf16[64,1,32]{0,2,1:T(8,128)(2,1)S(1)}, u32[]{:S(2)}, u32[]{:S(2)}) collective-permute-start(bf16[64,1,32]{0,2,1:T(8,128)(2,1)S(1)} %get-tuple-element.221), channel_id=1, source_target_pairs={{0,4},{4,8},{8,12},{1,5},{5,9},{9,13},{2,6},{6,10},{10,14},{3,7},{... | collective-permute-start | bytes 12296 | tf_op jit(solution)/shard_map/ppermute | solution.py:15
  206.1 4.0 %collective-permute-start.9 = (bf16[64,1,32]{0,2,1:T(8,128)(2,1)S(1)}, bf16[64,1,32]{0,2,1:T(8,128)(2,1)S(1)}, u32[]{:S(2)}, u32[]{:S(2)}) collective-permute-start(bf16[64,1,32]{0,2,1:T(8,128)(2,1)S(1)} %get-tuple-element.222), channel_id=1, source_target_pairs={{4,0},{8,4},{12,8},{5,1},{9,5},{13,9},{6,2},{10,6},{14,10},{7,3},{... | collective-permute-start | bytes 12296 | tf_op jit(solution)/shard_map/ppermute | solution.py:18
  211.0 6.5 %collective-permute-start.10 = (bf16[64,34,1]{0,2,1:T(2,128)(2,1)S(1)}, bf16[64,34,1]{0,2,1:T(2,128)(2,1)S(1)}, u32[]{:S(2)}, u32[]{:S(2)}) collective-permute-start(bf16[64,34,1]{0,2,1:T(2,128)(2,1)S(1)} %get-tuple-element.219), channel_id=1, source_target_pairs={{0,1},{1,2},{2,3},{4,5},{5,6},{6,7},{8,9},{9,10},{10,11},{12,13},{... | collective-permute-start | bytes 13064 | tf_op jit(solution)/shard_map/ppermute | solution.py:15
  214.4 5.6 %collective-permute-start.11 = (bf16[64,34,1]{0,2,1:T(2,128)(2,1)S(1)}, bf16[64,34,1]{0,2,1:T(2,128)(2,1)S(1)}, u32[]{:S(2)}, u32[]{:S(2)}) collective-permute-start(bf16[64,34,1]{0,2,1:T(2,128)(2,1)S(1)} %get-tuple-element.220), channel_id=1, source_target_pairs={{1,0},{2,1},{3,2},{5,4},{6,5},{7,6},{9,8},{10,9},{11,10},{13,12},{... | collective-permute-start | bytes 13064 | tf_op jit(solution)/shard_map/ppermute | solution.py:18
  226.5 15.1 %copy-start.2 = (f32[32,32]{1,0:T(8,128)}, f32[32,32]{1,0:T(8,128)S(1)}, u32[]{:S(2)}) copy-start(f32[32,32]{1,0:T(8,128)S(1)} %broadcast_add_fusion) | copy-start | bytes 12292
Sparse Core Ops, SparseCore 0:
  9.5 63.5 all-gather.1
where the time goes:
time: 250 us; the launch traced here: 248 us
  waiting for transfers between devices  80 us (32%)
  local copies, waits for them, and re-layouts  63.7 us (25%)
  starting transfers between devices  26 us (10%)
  matrix products  23.9 us (10%)
  between operations  17.1 us (7%)
  other arithmetic  16.3 us (7%)
  blocking collectives  14.3 us (6%)
  loops' own time  7.15 us (3%)
    all_gather x1, waiting for transfers between devices, body(): shards = lax.all_gather(ref_feats, 'qry', axis=1, tiled=True)  62.7 us
    dot_general x1, matrix products, frame_sims(): lax.dot_general(query_mat, ref_mat, (((1,), (1,)), ((), ())), preferred_e...  18.8 us
    ppermute x6, starting transfers between devices, padded_2(): lax.ppermute(lax.slice_in_dim(block, block.shape[dim] - width, None, axis...  18 us
    ppermute x6, waiting for transfers between devices, padded_2(): lax.ppermute(lax.slice_in_dim(block, 0, width, axis=dim), axis, backward)  16.2 us
    dot_general x1, local copies, waits for them, and re-layouts, frame_sims(): lax.dot_general(query_mat, ref_mat, (((1,), (1,)), ((), ())), preferred_e...  12.7 us
    reduce_max x8, other arithmetic, one_block(): jnp.max(result.reshape(outputs, block_rows // 2, 2, width // 2, 2), axis=...  12.3 us
    while x76, local copies, waits for them, and re-layouts  11.5 us
    concatenate x10, local copies, waits for them, and re-layouts, one_block(): jnp.concatenate([window[:, shift_row:shift_row + block_rows, shift_col:sh...  11 us
  transfers between devices with their start and end apart: 13, of which 8 were waited for; matrix products, arithmetic and copies ran while one was open for 2% of the time, Pallas kernels for 0%

commit v1 on v0

--- a/solution.py
+++ b/solution.py
@@ -106,7 +106,8 @@
         0
     ]
     chosen, picked = slot_table(own_mask, MOST)
-    shards = lax.all_gather(ref_feats, "qry", axis=1, tiled=True)
+    outgoing = jnp.stack([ref_feats] * lax.axis_size("qry"))
+    shards = jnp.concatenate(lax.all_to_all(outgoing, "qry", 0, 0), axis=1)
     senders = shards.shape[1]
     sims = frame_sims(query_mat, shards.reshape(tile_rows * senders * regions, channels), regions)
     sims = sims.reshape(1, frames, tile_rows, senders)

time: 250 us -> 283 us (1.13)
  waiting for transfers between devices: 80 us -> 113 us
  between operations: 17.1 us -> 3.67 us
  local copies, waits for them, and re-layouts: 63.7 us -> 70.2 us
  starting transfers between devices: 26 us -> 32.4 us
    all_to_all x0 -> x1, waiting for transfers between devices: none -> 96.2 us  [body(): shards = jnp.concatenate(lax.all_to_all(outgoing, 'qry', 0, 0), axis=1)]
    all_gather x1 -> x0, waiting for transfers between devices: 62.7 us -> none  [body(): shards = lax.all_gather(ref_feats, 'qry', axis=1, tiled=True)]
    reshape x0 -> x1, local copies, waits for them, and re-layouts: none -> 8.66 us  [body(): shards = jnp.concatenate(lax.all_to_all(outgoing, 'qry', 0, 0), axis=1)]
    all_gather x1 -> x0, local copies, waits for them, and re-layouts: 8.6 us -> none  [body(): shards = lax.all_gather(ref_feats, 'qry', axis=1, tiled=True)]
    another operation x0 -> x1, local copies, waits for them, and re-layouts: none -> 6.12 us  [body(): outgoing = jnp.stack([ref_feats] * lax.axis_size('qry'))]
    all_to_all x0 -> x1, starting transfers between devices: none -> 5.7 us  [body(): shards = jnp.concatenate(lax.all_to_all(outgoing, 'qry', 0, 0), axis=1)]
  transfers between devices with their start and end apart: 13 -> 13, of which waited for: 8 -> 8; matrix products, arithmetic and copies ran while one was open for 2% -> 1% of each run, Pallas kernels for 0% -> 0%
where the time goes in v1:
time: 283 us; the launch traced here: 281 us
  waiting for transfers between devices  113 us (40%)
  local copies, waits for them, and re-layouts  70.2 us (25%)
  starting transfers between devices  32.4 us (11%)
  matrix products  23.9 us (8%)
  other arithmetic  16.3 us (6%)
  blocking collectives  14.3 us (5%)
  loops' own time  7.39 us (3%)
  between operations  3.67 us (1%)
    all_to_all x1, waiting for transfers between devices, body(): shards = jnp.concatenate(lax.all_to_all(outgoing, 'qry', 0, 0), axis=1)  96.2 us
    dot_general x1, matrix products, frame_sims(): lax.dot_general(query_mat, ref_mat, (((1,), (1,)), ((), ())), preferred_e...  18.8 us
    ppermute x6, starting transfers between devices, padded_2(): lax.ppermute(lax.slice_in_dim(block, block.shape[dim] - width, None, axis...  18.8 us
    ppermute x6, waiting for transfers between devices, padded_2(): lax.ppermute(lax.slice_in_dim(block, 0, width, axis=dim), axis, backward)  16.2 us
    dot_general x1, local copies, waits for them, and re-layouts, frame_sims(): lax.dot_general(query_mat, ref_mat, (((1,), (1,)), ((), ())), preferred_e...  12.8 us
    reduce_max x8, other arithmetic, one_block(): jnp.max(result.reshape(outputs, block_rows // 2, 2, width // 2, 2), axis=...  12.3 us
    while x76, local copies, waits for them, and re-layouts  11.5 us
    concatenate x10, local copies, waits for them, and re-layouts, one_block(): jnp.concatenate([window[:, shift_row:shift_row + block_rows, shift_col:sh...  11 us
  transfers between devices with their start and end apart: 13, of which 8 were waited for; matrix products, arithmetic and copies ran while one was open for 1% of the time, Pallas kernels for 0%

profile of v1, /device:TPU:0, one launch (start us, length us, event | category | flops | bytes accessed | tf_op | source)
XLA Modules:
  0.0 281.1 jit_solution(12097397099688447556)
XLA Ops:
  0.6 6.1 %stack.2 = bf16[4,32,1,9,3840]{4,1,3,2,0:T(8,128)(2,1)} broadcast(bf16[32,9,3840]{2,0,1:T(8,128)(2,1)} %bitcast.125), dimensions={1,3,4} | broadcast | bytes 11059200 | tf_op jit(solution)/shard_map/stack | solution.py:109
  6.8 5.7 %all-to-all-start = ((bf16[4,32,1,9,3840]{4,1,3,2,0:T(8,128)(2,1)}), bf16[4,32,1,9,3840]{4,1,3,2,0:T(8,128)(2,1)}, u32[]{:S(2)}, u32[]{:S(2)}) async-start(bf16[4,32,1,9,3840]{4,1,3,2,0:T(8,128)(2,1)} %stack.2), calls=%async_computation | async-start | bytes 17694720 | tf_op jit(solution)/shard_map/all_to_all | solution.py:110
  15.1 96.2 %all-to-all-done = bf16[4,32,1,9,3840]{4,1,3,2,0:T(8,128)(2,1)} async-done(((bf16[4,32,1,9,3840]{4,1,3,2,0:T(8,128)(2,1)}), bf16[4,32,1,9,3840]{4,1,3,2,0:T(8,128)(2,1)}, u32[]{:S(2)}, u32[]{:S(2)}) %all-to-all-start) | async-done | bytes 8847392 | tf_op jit(solution)/shard_map/all_to_all | solution.py:110
  111.3 8.7 %copy.60 = bf16[32,4,1,9,3840]{4,1,0,3,2:T(4,128)(2,1)} copy(bf16[32,4,1,9,3840]{4,0,3,2,1:T(8,128)(2,1)} %bitcast.16) | data formatting | bytes 17694720 | tf_op jit(solution)/shard_map/reshape | solution.py:110
  119.9 12.8 %reshape.201 = bf16[128,9,3840,1]{2,0,1,3:T(8,128)(2,1)} reshape(bf16[32,4,1,9,3840]{4,1,0,3,2:T(4,128)(2,1)} %copy.60) | data formatting | bytes 17694720 | tf_op jit(solution)/shard_map/dot_general | solution.py:33
  132.7 18.8 %fusion.7 = f32[128,9,128]{2,0,1:T(8,128)S(1)} fusion(bf16[128,9,3840,1]{2,0,1,3:T(8,128)(2,1)} %reshape.201, bf16[128,9,3840]{2,0,1:T(8,128)(2,1)} %param.19), kind=kOutput, calls=%fused_computation.40 | convolution fusion | flops 10193338368 | bytes 18284544 | tf_op jit(solution)/shard_map/dot_general | solution.py:33
  156.1 4.8 %collective-permute-start.2 = (f32[130,1]{1,0:T(8,128)S(1)}, f32[130,1]{1,0:T(8,128)S(1)}, u32[]{:S(2)}, u32[]{:S(2)}) collective-permute-start(f32[130,1]{1,0:T(8,128)S(1)} %get-tuple-element.223), channel_id=1, source_target_pairs={{0,1},{1,2},{2,3},{4,5},{5,6},{6,7},{8,9},{9,10},{10,11},{12,13},{... | collective-permute-start | bytes 1568 | tf_op jit(solution)/shard_map/ppermute | solution.py:15
  162.9 4.3 %collective-permute-done.3 = f32[130,1]{1,0:T(8,128)S(1)} collective-permute-done((f32[130,1]{1,0:T(8,128)S(1)}, f32[130,1]{1,0:T(8,128)S(1)}, u32[]{:S(2)}, u32[]{:S(2)}) %collective-permute-start.3) | collective-permute-done | bytes 552 | tf_op jit(solution)/shard_map/ppermute | solution.py:18
  167.3 23.2 %while.30 = (s32[]{:T(128)}, bf16[4,32,16,64]{3,2,0,1:T(8,128)(2,1)S(1)}, s32[4]{0:T(128)S(1)}, f32[1,130,130]{2,1,0:T(8,128)S(1)}, f32[32,9]{0,1:T(8,128)S(1)},...) while((s32[]{:T(128)}, ...), condition=%wide.region_4.5_spmd, body=%wide.region_2.4_spmd.sunk | while | flops 14647306 | bytes 2885173 | solution.py:74
  170.4 2.5 reduce_max.42
  176.2 2.5 reduce_max.42
  182.0 2.5 reduce_max.42
  187.8 2.5 reduce_max.42
  190.5 2.8 collective-permute-start.4
  194.7 2.7 collective-permute-done.5
  198.2 3.5 %collective-permute-start.6 = (bf16[32,66,1]{1,0,2:T(8,128)(2,1)S(1)}, bf16[32,66,1]{1,0,2:T(8,128)(2,1)S(1)}, u32[]{:S(2)}, u32[]{:S(2)}) collective-permute-start(bf16[32,66,1]{1,0,2:T(8,128)(2,1)S(1)} %copy.62), channel_id=1, source_target_pairs={{0,1},{1,2},{2,3},{4,5},{5,6},{6,7},{8,9},{9,10},{10,11},{12,13},{... | collective-permute-start | bytes 12680 | tf_op jit(solution)/shard_map/ppermute | solution.py:15
  204.7 2.9 %collective-permute-done.7 = bf16[32,66,1]{1,0,2:T(8,128)(2,1)S(1)} collective-permute-done((bf16[32,66,1]{1,0,2:T(8,128)(2,1)S(1)}, bf16[32,66,1]{1,0,2:T(8,128)(2,1)S(1)}, u32[]{:S(2)}, u32[]{:S(2)}) %collective-permute-start.7) | collective-permute-done | bytes 4256 | tf_op jit(solution)/shard_map/ppermute | solution.py:18
  209.0 32.4 %while.31 = (s32[]{:T(128)}, bf16[4,64,8,32]{1,3,2,0:T(8,128)(2,1)}, s32[4]{0:T(128)S(1)}, bf16[32,66,66]{2,0,1:T(8,128)(2,1)S(1)}, bf16[64,288]{1,0:T(8,128)(2,...) while((s32[]{:T(128)}, ...), condition=%wide.region_7.8_spmd, body=%wide.region_5.7_spmd.sunk | while | flops 37994504 | bytes 4822013 | solution.py:74
  242.1 2.9 %collective-permute-start.8 = (bf16[64,1,32]{0,2,1:T(8,128)(2,1)S(1)}, bf16[64,1,32]{0,2,1:T(8,128)(2,1)S(1)}, u32[]{:S(2)}, u32[]{:S(2)}) collective-permute-start(bf16[64,1,32]{0,2,1:T(8,128)(2,1)S(1)} %get-tuple-element.221), channel_id=1, source_target_pairs={{0,4},{4,8},{8,12},{1,5},{5,9},{9,13},{2,6},{6,10},{10,14},{3,7},{... | collective-permute-start | bytes 12296 | tf_op jit(solution)/shard_map/ppermute | solution.py:15
  250.0 3.5 %collective-permute-start.10 = (bf16[64,34,1]{0,2,1:T(2,128)(2,1)S(1)}, bf16[64,34,1]{0,2,1:T(2,128)(2,1)S(1)}, u32[]{:S(2)}, u32[]{:S(2)}) collective-permute-start(bf16[64,34,1]{0,2,1:T(2,128)(2,1)S(1)} %get-tuple-element.219), channel_id=1, source_target_pairs={{0,1},{1,2},{2,3},{4,5},{5,6},{6,7},{8,9},{9,10},{10,11},{12,13},{... | collective-permute-start | bytes 13064 | tf_op jit(solution)/shard_map/ppermute | solution.py:15
  256.5 2.6 collective-permute-done.11
  260.3 5.3 %while.32 = (s32[]{:T(128)}, bf16[2,128,16,32]{1,3,2,0:T(8,128)(2,1)S(1)}, s32[2]{0:T(128)S(1)}, bf16[64,34,34]{0,2,1:T(8,128)(2,1)S(1)}, bf16[128,576]{1,0:T(8,...) while((s32[]{:T(128)}, ...), condition=%wide.region_9.10_spmd, body=%wide.region_8.9_spmd.sunk | while | flops 75694088 | bytes 3490551 | solution.py:74
  266.1 8.5 %pmax.7 = f32[32,2]{0,1:T(2,128)S(1)} all-reduce(f32[32,2]{0,1:T(2,128)S(1)} %select_reduce_fusion), channel_id=1, replica_groups=mesh['groups'=2,'qry'=4,'ref'=4] {'ref'}, use_global_device_ids=true, to_apply=%region_12.13 | all-reduce | flops 64 | bytes 512 | tf_op jit(solution)/shard_map/pmax | solution.py:145
  274.7 5.8 %psum.7 = f32[2]{0:T(128)S(1)} all-reduce(f32[2]{0:T(128)S(1)} %select_reduce_fusion.1), channel_id=1, replica_groups=mesh['groups'=2,'qry'=4,'ref'=4] {'qry'}, use_global_device_ids=true, to_apply=%region_14.15 | all-reduce | flops 2 | bytes 16 | tf_op jit(solution)/shard_map/psum | solution.py:148
  (207 shorter events, 67.4 us)
Async XLA Ops:
  0.6 264.9 %copy-start = (bf16[128]{0:T(256)(128)(2,1)S(1)}, bf16[128]{0:T(256)(128)(2,1)}, u32[]{:S(2)}) copy-start(bf16[128]{0:T(256)(128)(2,1)} %param.30) | copy-start | bytes 772
  6.8 104.5 %all-to-all-start = ((bf16[4,32,1,9,3840]{4,1,3,2,0:T(8,128)(2,1)}), bf16[4,32,1,9,3840]{4,1,3,2,0:T(8,128)(2,1)}, u32[]{:S(2)}, u32[]{:S(2)}) async-start(bf16[4,32,1,9,3840]{4,1,3,2,0:T(8,128)(2,1)} %stack.2), calls=%async_computation | async-start | bytes 17694720 | tf_op jit(solution)/shard_map/all_to_all | solution.py:110
  132.7 29.5 %copy-start.6 = (f32[3,3,32]{2,1,0:T(4,128)S(1)}, f32[3,3,32]{2,1,0:T(4,128)}, u32[]{:S(2)}) copy-start(f32[3,3,32]{2,1,0:T(4,128)} %param.24) | copy-start | bytes 3460
  132.7 29.6 %copy-start.7 = (s32[2]{0:T(128)S(1)}, s32[2]{0:T(128)}, u32[]{:S(2)}) copy-start(s32[2]{0:T(128)} %param.22) | copy-start | bytes 28
  132.7 34.6 %copy-start.5 = (f32[32]{0:T(128)S(1)}, f32[32]{0:T(128)}, u32[]{:S(2)}) copy-start(f32[32]{0:T(128)} %param.25) | copy-start | bytes 388
  151.6 2.6 collective-permute-start
  152.9 3.1 %collective-permute-start.1 = (f32[1,128]{1,0:T(1,128)S(1)}, f32[1,128]{1,0:T(1,128)S(1)}, u32[]{:S(2)}, u32[]{:S(2)}) collective-permute-start(f32[1,128]{1,0:T(1,128)S(1)} %get-tuple-element.226), channel_id=1, source_target_pairs={{4,0},{8,4},{12,8},{5,1},{9,5},{13,9},{6,2},{10,6},{14,10},{7,3},{... | collective-permute-start | bytes 1544 | tf_op jit(solution)/shard_map/ppermute | solution.py:18
  156.1 6.8 %collective-permute-start.2 = (f32[130,1]{1,0:T(8,128)S(1)}, f32[130,1]{1,0:T(8,128)S(1)}, u32[]{:S(2)}, u32[]{:S(2)}) collective-permute-start(f32[130,1]{1,0:T(8,128)S(1)} %get-tuple-element.223), channel_id=1, source_target_pairs={{0,1},{1,2},{2,3},{4,5},{5,6},{6,7},{8,9},{9,10},{10,11},{12,13},{... | collective-permute-start | bytes 1568 | tf_op jit(solution)/shard_map/ppermute | solution.py:15
  160.9 6.2 %collective-permute-start.3 = (f32[130,1]{1,0:T(8,128)S(1)}, f32[130,1]{1,0:T(8,128)S(1)}, u32[]{:S(2)}, u32[]{:S(2)}) collective-permute-start(f32[130,1]{1,0:T(8,128)S(1)} %get-tuple-element.224), channel_id=1, source_target_pairs={{1,0},{2,1},{3,2},{5,4},{6,5},{7,6},{9,8},{10,9},{11,10},{13,12},{... | collective-permute-start | bytes 1568 | tf_op jit(solution)/shard_map/ppermute | solution.py:18
  167.3 36.2 %copy-start.1 = (bf16[3,3,64,32]{2,3,1,0:T(8,128)(2,1)S(1)}, bf16[3,3,64,32]{2,3,1,0:T(8,128)(2,1)}, u32[]{:S(2)}) copy-start(bf16[3,3,64,32]{2,3,1,0:T(8,128)(2,1)} %param.26) | copy-start | bytes 110596
  190.5 18.6 %copy-start.3 = (f32[64]{0:T(128)S(1)}, f32[64]{0:T(128)}, u32[]{:S(2)}) copy-start(f32[64]{0:T(128)} %param.27) | copy-start | bytes 772
  190.5 4.1 %collective-permute-start.4 = (bf16[32,1,64]{2,1,0:T(2,128)(2,1)S(1)}, bf16[32,1,64]{2,1,0:T(2,128)(2,1)S(1)}, u32[]{:S(2)}, u32[]{:S(2)}) collective-permute-start(bf16[32,1,64]{2,1,0:T(2,128)(2,1)S(1)} %get-tuple-element.217), channel_id=1, source_target_pairs={{0,4},{4,8},{8,12},{1,5},{5,9},{9,13},{2,6},{6,10},{10,14},{3,7},{... | collective-permute-start | bytes 12296 | tf_op jit(solution)/shard_map/ppermute | solution.py:15
  193.3 4.1 %collective-permute-start.5 = (bf16[32,1,64]{2,1,0:T(2,128)(2,1)S(1)}, bf16[32,1,64]{2,1,0:T(2,128)(2,1)S(1)}, u32[]{:S(2)}, u32[]{:S(2)}) collective-permute-start(bf16[32,1,64]{2,1,0:T(2,128)(2,1)S(1)} %get-tuple-element.218), channel_id=1, source_target_pairs={{4,0},{8,4},{12,8},{5,1},{9,5},{13,9},{6,2},{10,6},{14,10},{7,3},{... | collective-permute-start | bytes 12296 | tf_op jit(solution)/shard_map/ppermute | solution.py:18
  198.2 5.5 %collective-permute-start.6 = (bf16[32,66,1]{1,0,2:T(8,128)(2,1)S(1)}, bf16[32,66,1]{1,0,2:T(8,128)(2,1)S(1)}, u32[]{:S(2)}, u32[]{:S(2)}) collective-permute-start(bf16[32,66,1]{1,0,2:T(8,128)(2,1)S(1)} %copy.62), channel_id=1, source_target_pairs={{0,1},{1,2},{2,3},{4,5},{5,6},{6,7},{8,9},{9,10},{10,11},{12,13},{... | collective-permute-start | bytes 12680 | tf_op jit(solution)/shard_map/ppermute | solution.py:15
  202.0 5.5 %collective-permute-start.7 = (bf16[32,66,1]{1,0,2:T(8,128)(2,1)S(1)}, bf16[32,66,1]{1,0,2:T(8,128)(2,1)S(1)}, u32[]{:S(2)}, u32[]{:S(2)}) collective-permute-start(bf16[32,66,1]{1,0,2:T(8,128)(2,1)S(1)} %copy.63), channel_id=1, source_target_pairs={{1,0},{2,1},{3,2},{5,4},{6,5},{7,6},{9,8},{10,9},{11,10},{13,12},{... | collective-permute-start | bytes 12680 | tf_op jit(solution)/shard_map/ppermute | solution.py:18
  209.0 51.2 %copy-start.4 = (f32[128]{0:T(128)S(1)}, f32[128]{0:T(128)}, u32[]{:S(2)}) copy-start(f32[128]{0:T(128)} %param.29) | copy-start | bytes 1540
  242.1 5.0 %collective-permute-start.8 = (bf16[64,1,32]{0,2,1:T(8,128)(2,1)S(1)}, bf16[64,1,32]{0,2,1:T(8,128)(2,1)S(1)}, u32[]{:S(2)}, u32[]{:S(2)}) collective-permute-start(bf16[64,1,32]{0,2,1:T(8,128)(2,1)S(1)} %get-tuple-element.221), channel_id=1, source_target_pairs={{0,4},{4,8},{8,12},{1,5},{5,9},{9,13},{2,6},{6,10},{10,14},{3,7},{... | collective-permute-start | bytes 12296 | tf_op jit(solution)/shard_map/ppermute | solution.py:15
  245.1 4.0 %collective-permute-start.9 = (bf16[64,1,32]{0,2,1:T(8,128)(2,1)S(1)}, bf16[64,1,32]{0,2,1:T(8,128)(2,1)S(1)}, u32[]{:S(2)}, u32[]{:S(2)}) collective-permute-start(bf16[64,1,32]{0,2,1:T(8,128)(2,1)S(1)} %get-tuple-element.222), channel_id=1, source_target_pairs={{4,0},{8,4},{12,8},{5,1},{9,5},{13,9},{6,2},{10,6},{14,10},{7,3},{... | collective-permute-start | bytes 12296 | tf_op jit(solution)/shard_map/ppermute | solution.py:18
  250.0 6.5 %collective-permute-start.10 = (bf16[64,34,1]{0,2,1:T(2,128)(2,1)S(1)}, bf16[64,34,1]{0,2,1:T(2,128)(2,1)S(1)}, u32[]{:S(2)}, u32[]{:S(2)}) collective-permute-start(bf16[64,34,1]{0,2,1:T(2,128)(2,1)S(1)} %get-tuple-element.219), channel_id=1, source_target_pairs={{0,1},{1,2},{2,3},{4,5},{5,6},{6,7},{8,9},{9,10},{10,11},{12,13},{... | collective-permute-start | bytes 13064 | tf_op jit(solution)/shard_map/ppermute | solution.py:15
  253.5 5.6 %collective-permute-start.11 = (bf16[64,34,1]{0,2,1:T(2,128)(2,1)S(1)}, bf16[64,34,1]{0,2,1:T(2,128)(2,1)S(1)}, u32[]{:S(2)}, u32[]{:S(2)}) collective-permute-start(bf16[64,34,1]{0,2,1:T(2,128)(2,1)S(1)} %get-tuple-element.220), channel_id=1, source_target_pairs={{1,0},{2,1},{3,2},{5,4},{6,5},{7,6},{9,8},{10,9},{11,10},{13,12},{... | collective-permute-start | bytes 13064 | tf_op jit(solution)/shard_map/ppermute | solution.py:18
  266.0 15.1 %copy-start.2 = (f32[32,32]{1,0:T(8,128)}, f32[32,32]{1,0:T(8,128)S(1)}, u32[]{:S(2)}) copy-start(f32[32,32]{1,0:T(8,128)S(1)} %broadcast_add_fusion) | copy-start | bytes 12292
